TPU v7x, 256 devices: a whole 4x4x8 slice. The times are simulated.
256 devices in a mesh: leaf: 32 (over x, y, core), mp: 8 (over z).
Axes of the slice: x: 4, y: 4, z: 8, core: 2. Of those that a mesh axis runs over, the one named last changes fastest.
Arguments:
- activations: bfloat16 [8192, 4096], P('leaf', 'mp'), may hold values from -6 to 6
- w_query: bfloat16 [4096, 2048], P(None, 'mp'), may hold values from -0.0625 to 0.0625
- w_key: bfloat16 [4096, 2048], P(None, 'mp'), may hold values from -0.0625 to 0.0625
- w_value: bfloat16 [4096, 2048], P(None, 'mp'), may hold values from -0.09375 to 0.09375
- w_out: bfloat16 [2048, 4096], P('mp'), may hold values from -0.70710678 to 0.70710678
- norm_gain: float32 [4096], P('mp'), may hold values from 0.1 to 1.9
- key_cache: bfloat16 [256, 256, 2048], P('leaf', None, 'mp'), may hold values from -6 to 6
- value_cache: bfloat16 [256, 256, 2048], P('leaf', None, 'mp'), may hold values from -6 to 6
- parent: int32 [256], replicated, may hold values from 0 to 255, as said below
- node_len: int32 [256], replicated, may hold values from 1 to 256, as said below
- req_leaf: int32 [128], replicated, may hold values from 0 to 255, as said below
Outputs:
- layer_out: bfloat16 [8192, 4096], P('leaf', 'mp')
Inputs may be any that keep to these rules, and one draw needn't show every extreme that they name: Exactly 4 nodes are their own parent (the roots); node n's cache is held by leaf index n // 8. Every request's leaf, its parent and that parent's parent are three distinct nodes, the last a root; no request's middle or leaf node is held by a leaf index that holds a root. `node_len`: every root has 256 live rows. `req_leaf`: over the 4 requests of one leaf index, the nodes of their paths counted with repetition lie at most 2 on any one holder, and their middle and leaf nodes at most 2; both bounds are reached on some holder for every leaf index.
All inputs are finite; a program needn't handle non-finite values.
Results may differ from a plain program's by a relative error of at most 0.03.
Values may be sent and summed in bfloat16 or wider, within the bound.
A program may use at most 128 MiB of HBM per device.

v0:
```python
import math
import jax
import jax.numpy as jnp
from jax import lax
from jax.sharding import PartitionSpec as P

D = 4096
HD = 128
TENANTS = 4
NODE_DEV = 8
REQ_LEN = 64
REQ_DEV = 4
rope_base = 500000.0
mask_value = -1e30
norm_eps = 1e-06


def rotate(values, positions):
    half_width = values.shape[-1] // 2
    inverse_freq = jnp.exp(
        jnp.arange(half_width, dtype=jnp.float32) * (-2.0 * math.log(rope_base) / values.shape[-1])
    )
    angles = positions.astype(jnp.float32)[:, None] * inverse_freq[None, :]
    cosine = jnp.cos(angles)[:, None, :]
    sine_part = jnp.sin(angles)[:, None, :]
    front_half = values[..., :half_width]
    back_half = values[..., half_width:]
    return jnp.concatenate(
        [front_half * cosine - back_half * sine_part, back_half * cosine + front_half * sine_part],
        axis=-1,
    )


def route_table(sender_nodes, leaf_count, capacity):
    holders = sender_nodes // NODE_DEV
    item_count = sender_nodes.shape[0]
    earlier = jnp.arange(item_count)[:, None] > jnp.arange(item_count)[None, :]
    same_holder = holders[:, None] == holders[None, :]
    ranks = jnp.sum(earlier & same_holder, axis=1)
    slot_table = (
        jnp.full((leaf_count, capacity), -1, jnp.int32).at[holders, ranks].set(sender_nodes)
    )
    return (holders, ranks, slot_table)


def node_attention(queries, keys, values, lengths, heads_local):
    blocks, row_total, width = queries.shape
    head_dim = width // heads_local
    query_heads = queries.reshape(blocks, row_total, heads_local, head_dim)
    key_heads = keys.reshape(blocks, keys.shape[1], heads_local, head_dim)
    value_heads = values.reshape(blocks, values.shape[1], heads_local, head_dim)
    scores = jnp.einsum(
        "nqhd,nkhd->nhqk", query_heads, key_heads, preferred_element_type=jnp.float32
    ) * head_dim ** (-0.5)
    live_mask = jnp.arange(keys.shape[1])[None, :] < lengths[:, None]
    scores = jnp.where(live_mask[:, None, None, :], scores, mask_value)
    highest = jnp.max(scores, axis=-1)
    weights = jnp.exp(scores - highest[..., None])
    totals = jnp.sum(weights, axis=-1)
    mixture = jnp.einsum(
        "nhqk,nkhd->nqhd",
        weights.astype(jnp.bfloat16),
        value_heads,
        preferred_element_type=jnp.float32,
    )
    result = (
        (mixture / jnp.transpose(totals, (0, 2, 1))[..., None])
        .astype(jnp.bfloat16)
        .reshape(blocks, row_total, width)
    )
    return (result, jnp.transpose(highest + jnp.log(totals), (0, 2, 1)))


def self_attention(queries, keys, values):
    head_dim = queries.shape[-1]
    row_total = queries.shape[1]
    scores = jnp.einsum(
        "rqhd,rkhd->rhqk", queries, keys, preferred_element_type=jnp.float32
    ) * head_dim ** (-0.5)
    causal = jnp.arange(row_total)[:, None] >= jnp.arange(row_total)[None, :]
    scores = jnp.where(causal[None, None], scores, mask_value)
    highest = jnp.max(scores, axis=-1)
    weights = jnp.exp(scores - highest[..., None])
    totals = jnp.sum(weights, axis=-1)
    mixture = jnp.einsum(
        "rhqk,rkhd->rqhd", weights.astype(jnp.bfloat16), values, preferred_element_type=jnp.float32
    )
    return (
        mixture / jnp.transpose(totals, (0, 2, 1))[..., None],
        jnp.transpose(highest + jnp.log(totals), (0, 2, 1)),
    )


def on_device(
    activations,
    w_query,
    w_key,
    w_value,
    w_out,
    norm_gain,
    key_cache,
    value_cache,
    parent,
    node_len,
    req_leaf,
):
    leaf_count = lax.axis_size("leaf")
    device = lax.axis_index("leaf")
    tok_rows = activations.shape[0]
    width_local = w_query.shape[1]
    heads_local = width_local // HD
    spread = leaf_count - TENANTS
    node_slots = 2 * ((REQ_DEV + spread - 1) // spread)
    all_slots = max(REQ_DEV // TENANTS, node_slots)
    columns = lax.all_gather(activations, "mp", axis=1, tiled=True)
    query_f, key_f, value_f = tuple(
        (
            jnp.dot(columns, matrix, preferred_element_type=jnp.float32)
            for matrix in (w_query, w_key, w_value)
        )
    )
    middle_all = parent[req_leaf]
    root_all = parent[middle_all]
    prefix = node_len[root_all] + node_len[middle_all] + node_len[req_leaf]
    mine_prefix = lax.dynamic_slice_in_dim(prefix, device * REQ_DEV, REQ_DEV)
    position = (mine_prefix[:, None] + jnp.arange(REQ_LEN, dtype=jnp.int32)[None, :]).reshape(
        tok_rows
    )
    queries = rotate(query_f.reshape(tok_rows, heads_local, HD), position).astype(jnp.bfloat16)
    keys = rotate(key_f.reshape(tok_rows, heads_local, HD), position).astype(jnp.bfloat16)
    values = value_f.astype(jnp.bfloat16)
    q_blocks = queries.reshape(REQ_DEV, REQ_LEN, width_local)
    self_out, self_lse = self_attention(
        queries.reshape(REQ_DEV, REQ_LEN, heads_local, HD),
        keys.reshape(REQ_DEV, REQ_LEN, heads_local, HD),
        values.reshape(REQ_DEV, REQ_LEN, heads_local, HD),
    )
    levels_all = jnp.stack([root_all, middle_all, req_leaf], axis=0).reshape(3, leaf_count, REQ_DEV)
    level_count = levels_all.shape[0]
    per_sender = jnp.transpose(levels_all, (1, 0, 2)).reshape(leaf_count, level_count * REQ_DEV)
    holders_all, ranks_all, tables = jax.vmap(
        lambda sender_nodes: route_table(sender_nodes, leaf_count, all_slots)
    )(per_sender)
    my_holder = holders_all[device]
    my_rank = ranks_all[device]
    item_request = jnp.arange(level_count * REQ_DEV) % REQ_DEV
    outgoing = (
        jnp.zeros((leaf_count, all_slots, REQ_LEN, width_local), jnp.bfloat16)
        .at[my_holder, my_rank]
        .set(q_blocks[item_request])
    )
    arrived = lax.all_to_all(outgoing, "leaf", split_axis=0, concat_axis=0, tiled=True)
    slot_nodes = tables[:, device].reshape(-1)
    filled = slot_nodes >= 0
    local_slot = jnp.where(filled, slot_nodes - device * NODE_DEV, 0)
    lengths = jnp.where(filled, node_len[jnp.maximum(slot_nodes, 0)], 0)
    node_out, node_lse = node_attention(
        arrived.reshape(leaf_count * all_slots, REQ_LEN, width_local),
        key_cache[local_slot],
        value_cache[local_slot],
        lengths,
        heads_local,
    )
    back_out = lax.all_to_all(
        node_out.reshape(leaf_count, all_slots, REQ_LEN, width_local),
        "leaf",
        split_axis=0,
        concat_axis=0,
        tiled=True,
    )
    back_lse = lax.all_to_all(
        node_lse.reshape(leaf_count, all_slots, REQ_LEN, heads_local).astype(jnp.bfloat16),
        "leaf",
        split_axis=0,
        concat_axis=0,
        tiled=True,
    ).astype(jnp.float32)
    got_out = back_out[my_holder, my_rank].reshape(level_count, REQ_DEV, REQ_LEN, width_local)
    got_lse = back_lse[my_holder, my_rank].reshape(level_count, REQ_DEV, REQ_LEN, heads_local)
    partial_out = jnp.concatenate(
        [got_out.reshape(3, REQ_DEV, REQ_LEN, heads_local, HD).astype(jnp.float32), self_out[None]],
        axis=0,
    )
    partial_lse = jnp.concatenate([got_lse, self_lse[None]], axis=0)
    highest = jnp.max(partial_lse, axis=0)
    factor = jnp.exp(partial_lse - highest[None])
    merged = jnp.sum(factor[..., None] * partial_out, axis=0) / jnp.sum(factor, axis=0)[..., None]
    attn = merged.astype(jnp.bfloat16).reshape(tok_rows, width_local)
    partial_value = jnp.dot(attn, w_out, preferred_element_type=jnp.float32)
    projected = lax.psum_scatter(
        partial_value.astype(jnp.bfloat16), "mp", scatter_dimension=1, tiled=True
    ).astype(jnp.float32)
    squares = lax.psum(jnp.sum(projected * projected, axis=1), "mp")
    row_scale = lax.rsqrt(squares / D + norm_eps)
    return (
        activations.astype(jnp.float32) + norm_gain[None, :] * projected * row_scale[:, None]
    ).astype(jnp.bfloat16)


def solution(mesh):
    in_specs = (
        P("leaf", "mp"),
        P(None, "mp"),
        P(None, "mp"),
        P(None, "mp"),
        P("mp", None),
        P("mp"),
        P("leaf", None, "mp"),
        P("leaf", None, "mp"),
        P(),
        P(),
        P(),
    )
    out_specs = P("leaf", "mp")
    return jax.shard_map(
        on_device, mesh=mesh, in_specs=in_specs, out_specs=out_specs, check_vma=False
    )
```

profile of v0, /device:TPU:4, one launch (start us, length us, event | category | flops | bytes accessed | tf_op | source)
XLA Modules:
  0.0 255.1 jit_solution(10342015116051803166)
XLA Ops:
  6.5 0.7 all-gather.2.cloned.1.call-update
  7.3 0.7 compare_select_fusion.8
  7.9 1.6 gather_fusion.5
  9.6 1.6 gather_fusion
  11.2 1.6 gather_fusion.1
  12.9 1.6 gather_fusion.4
  14.5 0.7 stack.14
  15.5 1.6 gather_fusion.3
  18.2 0.3 multiply_cosine_fusion
  18.5 34.5 %all-gather.2.cloned.1.call-done = bf16[256,4096]{1,0:T(8,128)(2,1)} async-done(((bf16[256,512]{1,0:T(8,128)(2,1)}), bf16[256,4096]{1,0:T(8,128)(2,1)}) %all-gather.2.cloned.1.call-update) | async-done | bytes 2097168 | tf_op jit(solution)/shard_map/all_gather | solution.py:115
  53.0 3.3 %fusion.69 = f32[256,256]{0,1:T(8,128)S(1)} fusion(bf16[256,4096]{1,0:T(8,128)(2,1)} %all-gather.2.cloned.1.call-done, bf16[4096,256]{1,0:T(8,128)(2,1)} %param.13), kind=kOutput, calls=%fused_computation.148 | convolution fusion | flops 536870912 | bytes 4456448 | tf_op jit(solution)/shard_map/dot_general | solution.py:118
  56.4 1.0 fusion.68
  57.7 0.6 gather_fusion.6
  58.3 1.6 broadcast_in_dim.33
  59.9 2.5 scatter_fusion
  62.4 7.5 %all-to-all-start = ((bf16[32,2,64,256]{3,2,1,0:T(8,128)(2,1)}), bf16[32,2,64,256]{3,2,1,0:T(8,128)(2,1)}, u32[]{:S(2)}, u32[]{:S(2)}) async-start(bf16[32,2,64,256]{3,2,1,0:T(8,128)(2,1)} %scatter_fusion), calls=%async_computation | async-start | bytes 4194304 | tf_op jit(solution)/shard_map/all_to_all | solution.py:152
  70.4 24.3 %scatter_fusion.1 = s32[32,32,2]{1,0,2:T(8,128)S(1)} fusion(s32[32,32,2]{1,0,2:T(8,128)S(1)} %broadcast_in_dim.30, s32[384]{0:T(512)S(1)} %reshape.587, s32[384]{0:T(512)S(1)} %reshape.589), kind=kCustom, calls=%fused_computation.12 | custom fusion | bytes 9216 | tf_op jit(solution)/shard_map/vmap()/scatter | solution.py:41
  94.9 0.3 copy.152
  95.3 0.3 copy.153
  95.7 0.8 gather_fusion.2
  96.5 0.3 copy.155
  97.0 5.3 %gather_fusion.7 = bf16[64,256,256]{2,1,0:T(8,128)(2,1)} fusion(bf16[8,256,256]{2,1,0:T(8,128)(2,1)S(1)} %copy-done.2, s32[1024]{0:T(1024)S(1)} %pad_clamp_fusion), kind=kCustom, calls=%fused_computation.7 | custom fusion | bytes 16777472 | tf_op jit(solution)/shard_map/gather | solution.py:159
  102.3 6.5 %gather_fusion.9 = bf16[64,256,256]{2,1,0:T(8,128)(2,1)} fusion(bf16[8,256,256]{2,1,0:T(8,128)(2,1)} %param.18, s32[1024]{0:T(1024)S(1)} %pad_clamp_fusion), kind=kCustom, calls=%fused_computation.9 | custom fusion | bytes 16777472 | tf_op jit(solution)/shard_map/gather | solution.py:160
  108.9 4.0 %reshape_reshape.7 = bf16[64,64,2,128]{3,2,1,0:T(2,128)(2,1)} reshape(bf16[32,2,64,256]{3,2,1,0:T(8,128)(2,1)} %all-to-all-done) | data formatting | bytes 4194304 | tf_op jit(solution)/shard_map/reshape;reshape | solution.py:49
  112.9 7.2 %fusion.6 = (f32[64,2,64]{2,1,0:T(2,128)S(1)}, f32[64,2,64,256]{3,2,1,0:T(8,128)S(1)}) fusion(pred[64,256]{1,0:T(8,128)(4,1)S(1)} %iota_compare_fusion, bf16[64,64,2,128]{3,2,1,0:T(2,128)(2,1)} %reshape_reshape.7, bf16[64,256,256]{2,1,0:T(8,128)(2,1)} %gather_fusion.7), kind=kOutput, calls=%fused_computation.21 | convolution fusion | flops 543154176 | bytes 18923520 | tf_op jit(solution)/shard_map/nqhd,nkhd->nhqk/dot_general | solution.py:52
  120.1 3.6 %fusion.8 = f32[64,2,64]{2,1,0:T(2,128)S(1)} fusion(f32[64,2,64,256]{3,2,1,0:T(8,128)S(1)} %get-tuple-element.25, f32[64,2,64]{2,1,0:T(2,128)S(1)} %get-tuple-element.24, pred[64,256]{1,0:T(8,128)(4,1)S(1)} %iota_compare_fusion), kind=kLoop, calls=%fused_computation.23 | loop fusion | flops 8380416 | bytes 8470528 | tf_op jit(solution)/shard_map/reduce_sum | solution.py:59
  123.7 0.7 reshape.599
  124.4 7.4 %all-to-all-start.1 = ((bf16[32,2,128]{2,1,0:T(2,128)(2,1)}), bf16[32,2,128]{2,1,0:T(2,128)(2,1)S(1)}, u32[]{:S(2)}, u32[]{:S(2)}) async-start(bf16[32,2,128]{2,1,0:T(2,128)(2,1)} %reshape.599), calls=%async_computation.1 | async-start | bytes 32768 | tf_op jit(solution)/shard_map/all_to_all | solution.py:171
  131.8 7.5 %fusion.10 = bf16[64,64,2,128]{3,1,2,0:T(8,128)(2,1)S(1)} fusion(f32[64,64,2]{1,2,0:T(2,128)S(1)} %bitcast.135, f32[64,2,64,256]{3,2,1,0:T(8,128)} %copy-done.3, f32[64,2,64]{2,1,0:T(2,128)S(1)} %get-tuple-element.24, pred[64,256]{1,0:T(8,128)(4,1)S(1)} %iota_compare_fusion, bf16[64,256,256]{2,1,0:T(8,128)(2,1)} %gather_fusion.9), kind=kOutput, calls=%fused_computation.26 | convolution fusion | flops 547356672 | bytes 18956288 | tf_op jit(solution)/shard_map/nhqk,nkhd->nqhd/dot_general | solution.py:60
  139.4 3.5 %copy.167 = bf16[64,64,2,128]{3,2,1,0:T(2,128)(2,1)} copy(bf16[64,64,2,128]{3,1,2,0:T(8,128)(2,1)S(1)} %fusion.10) | data formatting | bytes 4194304 | tf_op jit(solution)/shard_map/convert_element_type | solution.py:68
  142.9 4.4 %reshape_reshape.8 = bf16[32,2,64,256]{3,2,1,0:T(8,128)(2,1)} reshape(bf16[64,64,2,128]{3,2,1,0:T(2,128)(2,1)} %copy.167) | data formatting | bytes 4194304 | tf_op jit(solution)/shard_map/reshape;reshape | solution.py:165
  147.3 7.4 %all-to-all-start.2 = ((bf16[32,2,64,256]{3,2,1,0:T(8,128)(2,1)}), bf16[32,2,64,256]{3,2,1,0:T(8,128)(2,1)}, u32[]{:S(2)}, u32[]{:S(2)}) async-start(bf16[32,2,64,256]{3,2,1,0:T(8,128)(2,1)} %reshape_reshape.8), calls=%async_computation.2 | async-start | bytes 4194304 | tf_op jit(solution)/shard_map/all_to_all | solution.py:164
  155.9 2.9 %convolution_convert_fusion.1 = bf16[256,256]{1,0:T(8,128)(2,1)S(1)} fusion(bf16[256,4096]{1,0:T(8,128)(2,1)} %all-gather.2.cloned.1.call-done, bf16[4096,256]{1,0:T(8,128)(2,1)} %param.14), kind=kOutput, calls=%fused_computation.37 | convolution fusion | flops 536936448 | bytes 4325376 | tf_op jit(solution)/shard_map/dot_general | solution.py:118
  158.9 0.3 fusion.67
  159.2 0.2 fusion.18
  159.5 0.9 copy.170
  160.5 0.7 gather_fusion.8
  161.2 0.2 copy.165
  161.6 19.1 %all-to-all-done.2 = bf16[32,2,64,256]{3,2,1,0:T(8,128)(2,1)} async-done(((bf16[32,2,64,256]{3,2,1,0:T(8,128)(2,1)}), bf16[32,2,64,256]{3,2,1,0:T(8,128)(2,1)}, u32[]{:S(2)}, u32[]{:S(2)}) %all-to-all-start.2) | async-done | bytes 2097184 | tf_op jit(solution)/shard_map/all_to_all | solution.py:164
  180.7 3.0 %gather_fusion.10 = bf16[12,64,256]{2,1,0:T(8,128)(2,1)} fusion(bf16[32,2,64,256]{3,2,1,0:T(8,128)(2,1)} %all-to-all-done.2, s32[12]{0:T(128)S(1)} %get-tuple-element.20), kind=kCustom, calls=%fused_computation.10 | custom fusion | bytes 786528 | tf_op jit(solution)/shard_map/gather | solution.py:178
  183.7 1.4 reshape.496
  185.1 2.3 fusion.23
  187.4 0.3 divide_convert_fusion
  187.7 2.1 convolution_convert_fusion
  189.8 40.3 %reduce-scatter.2.cloned.1.call-done = bf16[256,512]{1,0:T(8,128)(2,1)} async-done(((bf16[256,4096]{1,0:T(8,128)(2,1)}), bf16[256,512]{1,0:T(8,128)(2,1)}) %reduce-scatter.2.cloned.1.call-update) | async-done | bytes 262160 | tf_op jit(solution)/shard_map/reduce_scatter | solution.py:190
  230.1 1.1 fusion.27
  231.2 15.3 %psum.7 = f32[256]{0:T(256)S(1)} all-reduce(f32[256]{0:T(256)S(1)} %fusion.27), channel_id=1, replica_groups=mesh['leaf'=32,'mp'=8] {'mp'}, use_global_device_ids=true, to_apply=%region_12.13 | all-reduce | flops 256 | bytes 2048 | tf_op jit(solution)/shard_map/psum | solution.py:193
  246.5 1.8 fusion.26
  (87 shorter events, 4.3 us)
Async XLA Ops:
  6.5 181.2 %copy-start = (bf16[256,4096]{1,0:T(8,128)(2,1)S(1)}, bf16[256,4096]{1,0:T(8,128)(2,1)}, u32[]{:S(2)}) copy-start(bf16[256,4096]{1,0:T(8,128)(2,1)} %param.15) | copy-start | bytes 6291460
  6.5 46.4 %all-gather.2.cloned.1.call-start = ((), (), s32[]{:S(2)}) async-start(), calls=%async_computation.4 | async-start | bytes 2359296 | tf_op jit(solution)/shard_map/all_gather | solution.py:115
  53.0 3.3 %copy-start.4 = (bf16[256,4096]{1,0:T(8,128)(2,1)S(1)}, bf16[256,4096]{1,0:T(8,128)(2,1)}, u32[]{:S(2)}) copy-start(bf16[256,4096]{1,0:T(8,128)(2,1)} %all-gather.2.cloned.1.call-done) | copy-start | bytes 6291460
  53.0 3.5 %copy-start.5 = (bf16[4096,256]{1,0:T(8,128)(2,1)S(1)}, bf16[4096,256]{1,0:T(8,128)(2,1)}, u32[]{:S(2)}) copy-start(bf16[4096,256]{1,0:T(8,128)(2,1)} %param.12) | copy-start | bytes 6291460
  62.4 46.5 %all-to-all-start = ((bf16[32,2,64,256]{3,2,1,0:T(8,128)(2,1)}), bf16[32,2,64,256]{3,2,1,0:T(8,128)(2,1)}, u32[]{:S(2)}, u32[]{:S(2)}) async-start(bf16[32,2,64,256]{3,2,1,0:T(8,128)(2,1)} %scatter_fusion), calls=%async_computation | async-start | bytes 4194304 | tf_op jit(solution)/shard_map/all_to_all | solution.py:152
  70.4 25.3 %copy-start.1 = (s32[256]{0:T(256)S(1)}, s32[256]{0:T(256)}, u32[]{:S(2)}) copy-start(s32[256]{0:T(256)} %param.20) | copy-start | bytes 3076
  70.4 26.6 %copy-start.2 = (bf16[8,256,256]{2,1,0:T(8,128)(2,1)S(1)}, bf16[8,256,256]{2,1,0:T(8,128)(2,1)}, u32[]{:S(2)}) copy-start(bf16[8,256,256]{2,1,0:T(8,128)(2,1)} %param.17) | copy-start | bytes 3145732
  120.1 3.6 %copy-start.3 = (f32[64,2,64,256]{3,2,1,0:T(8,128)}, f32[64,2,64,256]{3,2,1,0:T(8,128)S(1)}, u32[]{:S(2)}) copy-start(f32[64,2,64,256]{3,2,1,0:T(8,128)S(1)} %get-tuple-element.25) | copy-start | bytes 25165828
  124.4 22.8 %all-to-all-start.1 = ((bf16[32,2,128]{2,1,0:T(2,128)(2,1)}), bf16[32,2,128]{2,1,0:T(2,128)(2,1)S(1)}, u32[]{:S(2)}, u32[]{:S(2)}) async-start(bf16[32,2,128]{2,1,0:T(2,128)(2,1)} %reshape.599), calls=%async_computation.1 | async-start | bytes 32768 | tf_op jit(solution)/shard_map/all_to_all | solution.py:171
  147.3 33.4 %all-to-all-start.2 = ((bf16[32,2,64,256]{3,2,1,0:T(8,128)(2,1)}), bf16[32,2,64,256]{3,2,1,0:T(8,128)(2,1)}, u32[]{:S(2)}, u32[]{:S(2)}) async-start(bf16[32,2,64,256]{3,2,1,0:T(8,128)(2,1)} %reshape_reshape.8), calls=%async_computation.2 | async-start | bytes 4194304 | tf_op jit(solution)/shard_map/all_to_all | solution.py:164
  154.7 75.4 %reduce-scatter.2.cloned.1.call-start = ((), (), s32[]{:S(2)}) async-start(), calls=%async_computation.5 | async-start | bytes 2359296 | tf_op jit(solution)/shard_map/reduce_scatter | solution.py:190
  185.0 61.5 %copy-start.7 = (f32[512]{0:T(512)S(1)}, f32[512]{0:T(512)}, u32[]{:S(2)}) copy-start(f32[512]{0:T(512)} %param.16) | copy-start | bytes 6148
  187.4 59.1 %copy-start.6 = (bf16[256,512]{1,0:T(8,128)(2,1)S(1)}, bf16[256,512]{1,0:T(8,128)(2,1)}, u32[]{:S(2)}) copy-start(bf16[256,512]{1,0:T(8,128)(2,1)} %param.11) | copy-start | bytes 786436
Sparse Core Ops, SparseCore 0:
  9.1 43.7 all-gather.1
  189.9 40.1 reduce-scatter.1
where the time goes:
time: 256 us; the launch traced here: 255 us
  waiting for transfers between devices  94.6 us (37%)
  local copies, waits for them, and re-layouts  73.6 us (29%)
  matrix products  24.5 us (10%)
  starting transfers between devices  22.4 us (9%)
  blocking collectives  15.3 us (6%)
  between operations  13.9 us (5%)
  other arithmetic  10.8 us (4%)
    reduce_scatter x1, waiting for transfers between devices, on_device(): lax.psum_scatter(partial_value.astype(jnp.bfloat16), 'mp', scatter_dimens...  40.3 us
    all_gather x1, waiting for transfers between devices, on_device(): columns = lax.all_gather(activations, 'mp', axis=1, tiled=True)  34.5 us
    scatter x3, local copies, waits for them, and re-layouts, route_table(): jnp.full((leaf_count, capacity), -1, jnp.int32).at[holders, ranks]  24.5 us
    all_to_all x1, waiting for transfers between devices, on_device(): lax.all_to_all(node_out.reshape(leaf_count, all_slots, REQ_LEN, width_loc...  19.1 us
    psum x1, blocking collectives, on_device(): squares = lax.psum(jnp.sum(projected * projected, axis=1), 'mp')  15.3 us
    dot_general x1, matrix products, node_attention(): jnp.einsum('nhqk,nkhd->nqhd', weights.astype(jnp.bfloat16), value_heads,...  7.53 us
    all_to_all x1, starting transfers between devices, on_device(): lax.all_to_all(outgoing, 'leaf', split_axis=0, concat_axis=0, tiled=True)  7.5 us
    all_to_all x1, starting transfers between devices, on_device(): lax.all_to_all(node_out.reshape(leaf_count, all_slots, REQ_LEN, width_loc...  7.43 us
  transfers between devices with their start and end apart: 5, of which 3 were waited for; matrix products, arithmetic and copies ran while one was open for 28% of the time, Pallas kernels for 0%

commit v1 on v0

--- a/solution.py
+++ b/solution.py
@@ -13,6 +13,19 @@
 rope_base = 500000.0
 mask_value = -1e30
 norm_eps = 1e-06
+
+
+def gather_around(x, axis, dim):
+    ways = lax.axis_size(axis)
+    up = [(d, (d + 1) % ways) for d in range(ways)]
+    down = [(d, (d - 1) % ways) for d in range(ways)]
+    earlier, later = ([x], [x])
+    for _ in range(ways // 2):
+        earlier.append(lax.ppermute(earlier[-1], axis, up))
+    for _ in range((ways - 1) // 2):
+        later.append(lax.ppermute(later[-1], axis, down))
+    line = jnp.concatenate([*earlier[::-1], *later[1:]], axis=dim)
+    return jnp.roll(line, (lax.axis_index(axis) - ways // 2) * x.shape[dim], axis=dim)
 
 
 def rotate(values, positions):
@@ -112,7 +125,7 @@
     spread = leaf_count - TENANTS
     node_slots = 2 * ((REQ_DEV + spread - 1) // spread)
     all_slots = max(REQ_DEV // TENANTS, node_slots)
-    columns = lax.all_gather(activations, "mp", axis=1, tiled=True)
+    columns = gather_around(activations, "mp", 1)
     query_f, key_f, value_f = tuple(
         (
             jnp.dot(columns, matrix, preferred_element_type=jnp.float32)

time: 256 us -> 270 us (1.055)
  starting transfers between devices: 22.4 us -> 34.6 us
  local copies, waits for them, and re-layouts: 73.6 us -> 83.8 us
  waiting for transfers between devices: 94.6 us -> 86.7 us
    all_gather x1 -> x0, waiting for transfers between devices: 34.5 us -> none  [on_device(): columns = lax.all_gather(activations, 'mp', axis=1, tiled=True)]
    ppermute x0 -> x7, waiting for transfers between devices: none -> 17.4 us  [the longest x4 17.4 us: gather_around(): earlier.append(lax.ppermute(earlier[-1], axis, up))]
    ppermute x0 -> x7, starting transfers between devices: none -> 12.6 us  [the longest x3 10.6 us: gather_around(): later.append(lax.ppermute(later[-1], axis, down))]
    all_to_all x1, waiting for transfers between devices: 0.01 us -> 9.08 us  [on_device(): lax.all_to_all(outgoing, 'leaf', split_axis=0, concat_axis=0, tiled=True)]
    unnamed x18 -> x41, local copies, waits for them, and re-layouts: 0.98 us -> 7.04 us
  transfers between devices with their start and end apart: 5 -> 11, of which waited for: 3 -> 6; matrix products, arithmetic and copies ran while one was open for 28% -> 29% of each run, Pallas kernels for 0% -> 0%
where the time goes in v1:
time: 270 us; the launch traced here: 269 us
  waiting for transfers between devices  86.7 us (32%)
  local copies, waits for them, and re-layouts  83.8 us (31%)
  starting transfers between devices  34.6 us (13%)
  matrix products  22.2 us (8%)
  blocking collectives  15.2 us (6%)
  between operations  14.2 us (5%)
  other arithmetic  12.1 us (4%)
    reduce_scatter x1, waiting for transfers between devices, on_device(): lax.psum_scatter(partial_value.astype(jnp.bfloat16), 'mp', scatter_dimens...  41.3 us
    scatter x3, local copies, waits for them, and re-layouts, route_table(): jnp.full((leaf_count, capacity), -1, jnp.int32).at[holders, ranks]  24.5 us
    all_to_all x1, waiting for transfers between devices, on_device(): lax.all_to_all(node_out.reshape(leaf_count, all_slots, REQ_LEN, width_loc...  19 us
    ppermute x4, waiting for transfers between devices, gather_around(): earlier.append(lax.ppermute(earlier[-1], axis, up))  17.4 us
    psum x1, blocking collectives, on_device(): squares = lax.psum(jnp.sum(projected * projected, axis=1), 'mp')  15.2 us
    ppermute x3, starting transfers between devices, gather_around(): later.append(lax.ppermute(later[-1], axis, down))  10.6 us
    all_to_all x1, waiting for transfers between devices, on_device(): lax.all_to_all(outgoing, 'leaf', split_axis=0, concat_axis=0, tiled=True)  9.08 us
    all_to_all x1, starting transfers between devices, on_device(): lax.all_to_all(outgoing, 'leaf', split_axis=0, concat_axis=0, tiled=True)  7.67 us
  transfers between devices with their start and end apart: 11, of which 6 were waited for; matrix products, arithmetic and copies ran while one was open for 29% of the time, Pallas kernels for 0%

profile of v1, /device:TPU:4, one launch (start us, length us, event | category | flops | bytes accessed | tf_op | source)
XLA Modules:
  0.0 268.8 jit_solution(13134655070118880200)
XLA Ops:
  6.5 1.9 collective-permute-start
  8.5 3.9 %collective-permute-start.4 = (bf16[256,512]{1,0:T(8,128)(2,1)}, bf16[256,512]{1,0:T(8,128)(2,1)S(1)}, u32[]{:S(2)}, u32[]{:S(2)}) collective-permute-start(bf16[256,512]{1,0:T(8,128)(2,1)} %param.11), channel_id=1, source_target_pairs={{0,7},{1,0},{2,1},{3,2},{4,3},{5,4},{6,5},{7,6},{8,15},{9,8},{10,9... | collective-permute-start | bytes 786440 | tf_op jit(solution)/shard_map/ppermute | solution.py:26
  13.8 1.6 gather_fusion
  15.6 1.6 gather_fusion.1
  17.7 1.6 gather_fusion.5
  19.4 1.6 gather_fusion.4
  21.5 24.3 %scatter_fusion.1 = s32[32,32,2]{1,0,2:T(8,128)S(1)} fusion(s32[32,32,2]{1,0,2:T(8,128)S(1)} %broadcast_in_dim.30, s32[384]{0:T(512)S(1)} %reshape.587, s32[384]{0:T(512)S(1)} %reshape.589), kind=kCustom, calls=%fused_computation.12 | custom fusion | bytes 9216 | tf_op jit(solution)/shard_map/vmap()/scatter | solution.py:54
  47.0 1.3 gather_fusion.3
  48.8 8.6 %collective-permute-done.1 = bf16[256,512]{1,0:T(8,128)(2,1)S(1)} collective-permute-done((bf16[256,512]{1,0:T(8,128)(2,1)S(1)}, bf16[256,512]{1,0:T(8,128)(2,1)S(1)}, u32[]{:S(2)}, u32[]{:S(2)}) %collective-permute-start.1) | collective-permute-done | bytes 262176 | tf_op jit(solution)/shard_map/ppermute | solution.py:24
  57.5 3.2 %collective-permute-start.5 = (bf16[256,512]{1,0:T(8,128)(2,1)S(1)}, bf16[256,512]{1,0:T(8,128)(2,1)}, u32[]{:S(2)}, u32[]{:S(2)}) collective-permute-start(bf16[256,512]{1,0:T(8,128)(2,1)S(1)} %collective-permute-done.4), channel_id=1, source_target_pairs={{0,7},{1,0},{2,1},{3,2},{4,3},{5,4},{6,5},{7,6},{8,15},{9,8},{10,9... | collective-permute-start | bytes 786440 | tf_op jit(solution)/shard_map/ppermute | solution.py:26
  60.7 4.8 %collective-permute-done.2 = bf16[256,512]{1,0:T(8,128)(2,1)} collective-permute-done((bf16[256,512]{1,0:T(8,128)(2,1)S(1)}, bf16[256,512]{1,0:T(8,128)(2,1)}, u32[]{:S(2)}, u32[]{:S(2)}) %collective-permute-start.2) | collective-permute-done | bytes 262176 | tf_op jit(solution)/shard_map/ppermute | solution.py:24
  66.0 3.5 %collective-permute-start.6 = (bf16[256,512]{1,0:T(8,128)(2,1)}, bf16[256,512]{1,0:T(8,128)(2,1)S(1)}, u32[]{:S(2)}, u32[]{:S(2)}) collective-permute-start(bf16[256,512]{1,0:T(8,128)(2,1)} %collective-permute-done.5), channel_id=1, source_target_pairs={{0,7},{1,0},{2,1},{3,2},{4,3},{5,4},{6,5},{7,6},{8,15},{9,8},{10,9... | collective-permute-start | bytes 786440 | tf_op jit(solution)/shard_map/ppermute | solution.py:26
  69.5 4.0 %collective-permute-done.3 = bf16[256,512]{1,0:T(8,128)(2,1)} collective-permute-done((bf16[256,512]{1,0:T(8,128)(2,1)}, bf16[256,512]{1,0:T(8,128)(2,1)}, u32[]{:S(2)}, u32[]{:S(2)}) %collective-permute-start.3) | collective-permute-done | bytes 262176 | tf_op jit(solution)/shard_map/ppermute | solution.py:24
  73.5 1.0 constant_dynamic-update-slice_fusion.15
  74.5 1.0 constant_dynamic-update-slice_fusion.14
  75.6 1.0 constant_dynamic-update-slice_fusion.9
  76.6 1.0 constant_dynamic-update-slice_fusion.7
  77.6 1.1 constant_dynamic-update-slice_fusion.6
  78.8 1.0 constant_dynamic-update-slice_fusion.1
  80.9 1.0 fusion.20
  82.8 1.3 gather_fusion.6
  84.1 1.6 broadcast_in_dim.33
  85.7 2.8 %scatter_fusion = bf16[32,2,64,256]{3,2,1,0:T(8,128)(2,1)} fusion(bf16[32,2,64,256]{3,2,1,0:T(8,128)(2,1)} %broadcast_in_dim.33, s32[12]{0:T(128)S(1)} %get-tuple-element.21, bf16[12,64,256]{2,1,0:T(8,128)(2,1)} %gather_fusion.6), kind=kCustom, calls=%fused_computation.11 | custom fusion | bytes 1179744 | tf_op jit(solution)/shard_map/scatter | solution.py:163
  88.6 7.7 %all-to-all-start = ((bf16[32,2,64,256]{3,2,1,0:T(8,128)(2,1)}), bf16[32,2,64,256]{3,2,1,0:T(8,128)(2,1)}, u32[]{:S(2)}, u32[]{:S(2)}) async-start(bf16[32,2,64,256]{3,2,1,0:T(8,128)(2,1)} %scatter_fusion), calls=%async_computation | async-start | bytes 4194304 | tf_op jit(solution)/shard_map/all_to_all | solution.py:165
  96.2 1.0 copy.152
  98.7 1.6 copy.155
  101.2 5.3 %gather_fusion.7 = bf16[64,256,256]{2,1,0:T(8,128)(2,1)} fusion(bf16[8,256,256]{2,1,0:T(8,128)(2,1)S(1)} %copy-done.2, s32[1024]{0:T(1024)S(1)} %pad_clamp_fusion), kind=kCustom, calls=%fused_computation.7 | custom fusion | bytes 16777472 | tf_op jit(solution)/shard_map/gather | solution.py:172
  106.5 6.5 %gather_fusion.9 = bf16[64,256,256]{2,1,0:T(8,128)(2,1)} fusion(bf16[8,256,256]{2,1,0:T(8,128)(2,1)} %param.18, s32[1024]{0:T(1024)S(1)} %pad_clamp_fusion), kind=kCustom, calls=%fused_computation.9 | custom fusion | bytes 16777472 | tf_op jit(solution)/shard_map/gather | solution.py:173
  113.1 9.1 %all-to-all-done = bf16[32,2,64,256]{3,2,1,0:T(8,128)(2,1)} async-done(((bf16[32,2,64,256]{3,2,1,0:T(8,128)(2,1)}), bf16[32,2,64,256]{3,2,1,0:T(8,128)(2,1)}, u32[]{:S(2)}, u32[]{:S(2)}) %all-to-all-start) | async-done | bytes 2097184 | tf_op jit(solution)/shard_map/all_to_all | solution.py:165
  122.2 4.0 %reshape_reshape.7 = bf16[64,64,2,128]{3,2,1,0:T(2,128)(2,1)} reshape(bf16[32,2,64,256]{3,2,1,0:T(8,128)(2,1)} %all-to-all-done) | data formatting | bytes 4194304 | tf_op jit(solution)/shard_map/reshape;reshape | solution.py:62
  126.2 7.2 %fusion.6 = (f32[64,2,64]{2,1,0:T(2,128)S(1)}, f32[64,2,64,256]{3,2,1,0:T(8,128)S(1)}) fusion(pred[64,256]{1,0:T(8,128)(4,1)S(1)} %iota_compare_fusion, bf16[64,64,2,128]{3,2,1,0:T(2,128)(2,1)} %reshape_reshape.7, bf16[64,256,256]{2,1,0:T(8,128)(2,1)} %gather_fusion.7), kind=kOutput, calls=%fused_computation.21 | convolution fusion | flops 543154176 | bytes 18923520 | tf_op jit(solution)/shard_map/nqhd,nkhd->nhqk/dot_general | solution.py:65
  133.4 3.6 %fusion.8 = f32[64,2,64]{2,1,0:T(2,128)S(1)} fusion(f32[64,2,64,256]{3,2,1,0:T(8,128)S(1)} %get-tuple-element.25, f32[64,2,64]{2,1,0:T(2,128)S(1)} %get-tuple-element.24, pred[64,256]{1,0:T(8,128)(4,1)S(1)} %iota_compare_fusion), kind=kLoop, calls=%fused_computation.23 | loop fusion | flops 8380416 | bytes 8470528 | tf_op jit(solution)/shard_map/reduce_sum | solution.py:72
  137.7 6.8 %all-to-all-start.1 = ((bf16[32,2,128]{2,1,0:T(2,128)(2,1)}), bf16[32,2,128]{2,1,0:T(2,128)(2,1)S(1)}, u32[]{:S(2)}, u32[]{:S(2)}) async-start(bf16[32,2,128]{2,1,0:T(2,128)(2,1)} %reshape.599), calls=%async_computation.1 | async-start | bytes 32768 | tf_op jit(solution)/shard_map/all_to_all | solution.py:184
  144.6 7.5 %fusion.10 = bf16[64,64,2,128]{3,1,2,0:T(8,128)(2,1)S(1)} fusion(f32[64,64,2]{1,2,0:T(2,128)S(1)} %bitcast.132, f32[64,2,64,256]{3,2,1,0:T(8,128)} %copy-done.3, f32[64,2,64]{2,1,0:T(2,128)S(1)} %get-tuple-element.24, pred[64,256]{1,0:T(8,128)(4,1)S(1)} %iota_compare_fusion, bf16[64,256,256]{2,1,0:T(8,128)(2,1)} %gather_fusion.9), kind=kOutput, calls=%fused_computation.26 | convolution fusion | flops 547356672 | bytes 18956288 | tf_op jit(solution)/shard_map/nhqk,nkhd->nqhd/dot_general | solution.py:73
  152.1 3.5 %copy.167 = bf16[64,64,2,128]{3,2,1,0:T(2,128)(2,1)} copy(bf16[64,64,2,128]{3,1,2,0:T(8,128)(2,1)S(1)} %fusion.10) | data formatting | bytes 4194304 | tf_op jit(solution)/shard_map/convert_element_type | solution.py:81
  155.6 4.4 %reshape_reshape.8 = bf16[32,2,64,256]{3,2,1,0:T(8,128)(2,1)} reshape(bf16[64,64,2,128]{3,2,1,0:T(2,128)(2,1)} %copy.167) | data formatting | bytes 4194304 | tf_op jit(solution)/shard_map/reshape;reshape | solution.py:178
  160.0 7.5 %all-to-all-start.2 = ((bf16[32,2,64,256]{3,2,1,0:T(8,128)(2,1)}), bf16[32,2,64,256]{3,2,1,0:T(8,128)(2,1)}, u32[]{:S(2)}, u32[]{:S(2)}) async-start(bf16[32,2,64,256]{3,2,1,0:T(8,128)(2,1)} %reshape_reshape.8), calls=%async_computation.2 | async-start | bytes 4194304 | tf_op jit(solution)/shard_map/all_to_all | solution.py:177
  168.6 2.9 %fusion.25 = bf16[256,256]{1,0:T(8,128)(2,1)S(1)} fusion(bf16[4096,256]{1,0:T(8,128)(2,1)} %param.14, bf16[256,8192]{1,0:T(8,128)(2,1)} %copy-done.4, s32[]{:T(128)S(6)} %select_n.186), kind=kOutput, calls=%fused_computation.43 | convolution fusion | flops 536936448 | bytes 4325380 | tf_op jit(solution)/shard_map/dot_general | solution.py:131
  173.3 1.0 copy.165
  174.5 19.0 %all-to-all-done.2 = bf16[32,2,64,256]{3,2,1,0:T(8,128)(2,1)} async-done(((bf16[32,2,64,256]{3,2,1,0:T(8,128)(2,1)}), bf16[32,2,64,256]{3,2,1,0:T(8,128)(2,1)}, u32[]{:S(2)}, u32[]{:S(2)}) %all-to-all-start.2) | async-done | bytes 2097184 | tf_op jit(solution)/shard_map/all_to_all | solution.py:177
  193.4 3.0 %gather_fusion.10 = bf16[12,64,256]{2,1,0:T(8,128)(2,1)} fusion(bf16[32,2,64,256]{3,2,1,0:T(8,128)(2,1)} %all-to-all-done.2, s32[12]{0:T(128)S(1)} %get-tuple-element.20), kind=kCustom, calls=%fused_computation.10 | custom fusion | bytes 786528 | tf_op jit(solution)/shard_map/gather | solution.py:191
  196.4 1.4 reshape.496
  197.8 2.4 fusion.32
  200.5 2.1 convolution_convert_fusion
  202.6 41.3 %reduce-scatter.2.cloned.1.call-done = bf16[256,512]{1,0:T(8,128)(2,1)} async-done(((bf16[256,4096]{1,0:T(8,128)(2,1)}), bf16[256,512]{1,0:T(8,128)(2,1)}) %reduce-scatter.2.cloned.1.call-update) | async-done | bytes 262160 | tf_op jit(solution)/shard_map/reduce_scatter | solution.py:203
  243.9 1.1 fusion.36
  245.0 15.2 %psum.7 = f32[256]{0:T(256)S(1)} all-reduce(f32[256]{0:T(256)S(1)} %fusion.36), channel_id=1, replica_groups=mesh['leaf'=32,'mp'=8] {'mp'}, use_global_device_ids=true, to_apply=%region_12.13 | all-reduce | flops 256 | bytes 2048 | tf_op jit(solution)/shard_map/psum | solution.py:206
  260.1 1.8 fusion.35
  (121 shorter events, 13.2 us)
Async XLA Ops:
  6.5 193.9 %copy-start = (bf16[256,4096]{1,0:T(8,128)(2,1)S(1)}, bf16[256,4096]{1,0:T(8,128)(2,1)}, u32[]{:S(2)}) copy-start(bf16[256,4096]{1,0:T(8,128)(2,1)} %param.15) | copy-start | bytes 6291460
  6.5 41.7 %collective-permute-start = (bf16[256,512]{1,0:T(8,128)(2,1)}, bf16[256,512]{1,0:T(8,128)(2,1)S(1)}, u32[]{:S(2)}, u32[]{:S(2)}) collective-permute-start(bf16[256,512]{1,0:T(8,128)(2,1)} %param.11), channel_id=1, source_target_pairs={{0,1},{1,2},{2,3},{3,4},{4,5},{5,6},{6,7},{7,0},{8,9},{9,10},{10,1... | collective-permute-start | bytes 786440 | tf_op jit(solution)/shard_map/ppermute | solution.py:24
  8.5 49.1 %collective-permute-start.4 = (bf16[256,512]{1,0:T(8,128)(2,1)}, bf16[256,512]{1,0:T(8,128)(2,1)S(1)}, u32[]{:S(2)}, u32[]{:S(2)}) collective-permute-start(bf16[256,512]{1,0:T(8,128)(2,1)} %param.11), channel_id=1, source_target_pairs={{0,7},{1,0},{2,1},{3,2},{4,3},{5,4},{6,5},{7,6},{8,15},{9,8},{10,9... | collective-permute-start | bytes 786440 | tf_op jit(solution)/shard_map/ppermute | solution.py:26
  21.5 25.5 %copy-start.1 = (s32[256]{0:T(256)S(1)}, s32[256]{0:T(256)}, u32[]{:S(2)}) copy-start(s32[256]{0:T(256)} %param.20) | copy-start | bytes 3076
  21.5 54.0 %copy-start.5 = (bf16[256,512]{1,0:T(8,128)(2,1)S(1)}, bf16[256,512]{1,0:T(8,128)(2,1)}, u32[]{:S(2)}) copy-start(bf16[256,512]{1,0:T(8,128)(2,1)} %param.11) | copy-start | bytes 786436
  48.3 9.1 %collective-permute-start.1 = (bf16[256,512]{1,0:T(8,128)(2,1)S(1)}, bf16[256,512]{1,0:T(8,128)(2,1)S(1)}, u32[]{:S(2)}, u32[]{:S(2)}) collective-permute-start(bf16[256,512]{1,0:T(8,128)(2,1)S(1)} %collective-permute-done), channel_id=1, source_target_pairs={{0,1},{1,2},{2,3},{3,4},{4,5},{5,6},{6,7},{7,0},{8,9},{9,10},{10,1... | collective-permute-start | bytes 786440 | tf_op jit(solution)/shard_map/ppermute | solution.py:24
  57.3 8.2 %collective-permute-start.2 = (bf16[256,512]{1,0:T(8,128)(2,1)S(1)}, bf16[256,512]{1,0:T(8,128)(2,1)}, u32[]{:S(2)}, u32[]{:S(2)}) collective-permute-start(bf16[256,512]{1,0:T(8,128)(2,1)S(1)} %collective-permute-done.1), channel_id=1, source_target_pairs={{0,1},{1,2},{2,3},{3,4},{4,5},{5,6},{6,7},{7,0},{8,9},{9,10},{10,1... | collective-permute-start | bytes 786440 | tf_op jit(solution)/shard_map/ppermute | solution.py:24
  57.5 8.5 %collective-permute-start.5 = (bf16[256,512]{1,0:T(8,128)(2,1)S(1)}, bf16[256,512]{1,0:T(8,128)(2,1)}, u32[]{:S(2)}, u32[]{:S(2)}) collective-permute-start(bf16[256,512]{1,0:T(8,128)(2,1)S(1)} %collective-permute-done.4), channel_id=1, source_target_pairs={{0,7},{1,0},{2,1},{3,2},{4,3},{5,4},{6,5},{7,6},{8,15},{9,8},{10,9... | collective-permute-start | bytes 786440 | tf_op jit(solution)/shard_map/ppermute | solution.py:26
  65.6 7.9 %collective-permute-start.3 = (bf16[256,512]{1,0:T(8,128)(2,1)}, bf16[256,512]{1,0:T(8,128)(2,1)}, u32[]{:S(2)}, u32[]{:S(2)}) collective-permute-start(bf16[256,512]{1,0:T(8,128)(2,1)} %collective-permute-done.2), channel_id=1, source_target_pairs={{0,1},{1,2},{2,3},{3,4},{4,5},{5,6},{6,7},{7,0},{8,9},{9,10},{10,1... | collective-permute-start | bytes 786440 | tf_op jit(solution)/shard_map/ppermute | solution.py:24
  66.0 13.9 %copy-start.6 = (bf16[4096,256]{1,0:T(8,128)(2,1)S(1)}, bf16[4096,256]{1,0:T(8,128)(2,1)}, u32[]{:S(2)}) copy-start(bf16[4096,256]{1,0:T(8,128)(2,1)} %param.13) | copy-start | bytes 6291460
  66.0 10.5 %collective-permute-start.6 = (bf16[256,512]{1,0:T(8,128)(2,1)}, bf16[256,512]{1,0:T(8,128)(2,1)S(1)}, u32[]{:S(2)}, u32[]{:S(2)}) collective-permute-start(bf16[256,512]{1,0:T(8,128)(2,1)} %collective-permute-done.5), channel_id=1, source_target_pairs={{0,7},{1,0},{2,1},{3,2},{4,3},{5,4},{6,5},{7,6},{8,15},{9,8},{10,9... | collective-permute-start | bytes 786440 | tf_op jit(solution)/shard_map/ppermute | solution.py:26
  77.6 3.3 %copy-start.7 = (bf16[4096,256]{1,0:T(8,128)(2,1)S(1)}, bf16[4096,256]{1,0:T(8,128)(2,1)}, u32[]{:S(2)}) copy-start(bf16[4096,256]{1,0:T(8,128)(2,1)} %param.12) | copy-start | bytes 6291460
  79.9 2.0 copy-start.4
  84.1 17.1 %copy-start.2 = (bf16[8,256,256]{2,1,0:T(8,128)(2,1)S(1)}, bf16[8,256,256]{2,1,0:T(8,128)(2,1)}, u32[]{:S(2)}) copy-start(bf16[8,256,256]{2,1,0:T(8,128)(2,1)} %param.17) | copy-start | bytes 3145732
  88.6 33.6 %all-to-all-start = ((bf16[32,2,64,256]{3,2,1,0:T(8,128)(2,1)}), bf16[32,2,64,256]{3,2,1,0:T(8,128)(2,1)}, u32[]{:S(2)}, u32[]{:S(2)}) async-start(bf16[32,2,64,256]{3,2,1,0:T(8,128)(2,1)} %scatter_fusion), calls=%async_computation | async-start | bytes 4194304 | tf_op jit(solution)/shard_map/all_to_all | solution.py:165
  106.5 6.5 %copy-start.11 = (pred[64]{0:T(512)(128)(4,1)S(1)}, pred[64]{0:T(512)(128)(4,1)}, u32[]{:S(2)}) copy-start(pred[64]{0:T(512)(128)(4,1)} %ge.35) | copy-start | bytes 196
  133.4 3.6 %copy-start.3 = (f32[64,2,64,256]{3,2,1,0:T(8,128)}, f32[64,2,64,256]{3,2,1,0:T(8,128)S(1)}, u32[]{:S(2)}) copy-start(f32[64,2,64,256]{3,2,1,0:T(8,128)S(1)} %get-tuple-element.25) | copy-start | bytes 25165828
  137.7 22.2 %all-to-all-start.1 = ((bf16[32,2,128]{2,1,0:T(2,128)(2,1)}), bf16[32,2,128]{2,1,0:T(2,128)(2,1)S(1)}, u32[]{:S(2)}, u32[]{:S(2)}) async-start(bf16[32,2,128]{2,1,0:T(2,128)(2,1)} %reshape.599), calls=%async_computation.1 | async-start | bytes 32768 | tf_op jit(solution)/shard_map/all_to_all | solution.py:184
  155.5 12.2 %copy-start.9 = (bf16[256,2,64]{0,2,1:T(8,128)(2,1)S(1)}, bf16[256,2,64]{0,2,1:T(8,128)(2,1)}, u32[]{:S(2)}) copy-start(bf16[256,2,64]{0,2,1:T(8,128)(2,1)} %get-tuple-element.10) | copy-start | bytes 196612
  155.5 12.5 %copy-start.8 = (bf16[256,2,64]{0,2,1:T(8,128)(2,1)S(1)}, bf16[256,2,64]{0,2,1:T(8,128)(2,1)}, u32[]{:S(2)}) copy-start(bf16[256,2,64]{0,2,1:T(8,128)(2,1)} %get-tuple-element.9) | copy-start | bytes 196612
  160.0 33.4 %all-to-all-start.2 = ((bf16[32,2,64,256]{3,2,1,0:T(8,128)(2,1)}), bf16[32,2,64,256]{3,2,1,0:T(8,128)(2,1)}, u32[]{:S(2)}, u32[]{:S(2)}) async-start(bf16[32,2,64,256]{3,2,1,0:T(8,128)(2,1)} %reshape_reshape.8), calls=%async_computation.2 | async-start | bytes 4194304 | tf_op jit(solution)/shard_map/all_to_all | solution.py:177
  167.4 76.4 %reduce-scatter.2.cloned.1.call-start = ((), (), s32[]{:S(2)}) async-start(), calls=%async_computation.4 | async-start | bytes 2359296 | tf_op jit(solution)/shard_map/reduce_scatter | solution.py:203
  197.7 62.4 %copy-start.10 = (f32[512]{0:T(512)S(1)}, f32[512]{0:T(512)}, u32[]{:S(2)}) copy-start(f32[512]{0:T(512)} %param.16) | copy-start | bytes 6148
Sparse Core Ops, SparseCore 0:
  202.7 41.1 reduce-scatter.1
